TPU v7x, 128 devices: a whole 4x4x4 slice. The times are simulated.
128 devices in a mesh: au: 8 (over z_hi, y), pa: 8 (over x, z_lo), dev: 2 (over core).
Axes of the slice: x: 4, y: 4, z: 4 (z_hi: 2, z_lo: 2; z = z_hi * 2 + z_lo), core: 2. Of those that a mesh axis runs over, the one named last changes fastest.
Arguments:
- features: bfloat16 [8192, 64, 256], P('au', 'pa'), may hold values from -6 to 6
- item_ids: int32 [8192, 64], P('au', 'pa'), may hold values from 0 to 4095
- item_table: bfloat16 [4096, 256], replicated, may hold values from -4 to 4
- lengths: int32 [8192], P('au'), may hold values from 1 to 64
- routing_seed: int32 [4, 64], replicated, may hold values from 0 to 15
- w_qkv: bfloat16 [3, 256, 256], P(None, None, 'dev'), may hold values from -0.375 to 0.375
- w_out: bfloat16 [256, 256], P('dev'), may hold values from -0.375 to 0.375
- w_bilinear: bfloat16 [256, 256], P(None, 'dev'), may hold values from -0.375 to 0.375
- w_up: bfloat16 [256, 1024], P(None, 'dev'), may hold values from -0.375 to 0.375
- w_down: bfloat16 [1024, 256], P('dev'), may hold values from -0.1875 to 0.1875
Outputs:
- capsules: float32 [8192, 4, 256], P(('au', 'pa'), None, 'dev')
All inputs are finite; a program needn't handle non-finite values.
Results may differ from a plain program's by a relative error of at most 0.012.
The roundings to bfloat16 on the way count: a program that leaves them out, or rounds other values in their place, can miss the bound.
Values may be sent and summed in bfloat16 or wider, within the bound.
No kernel may reach another device: no remote copies, remote signals or barrier semaphores. Data moves between devices by JAX's collectives and lax.ppermute only.
A program may use at most 128 MiB of HBM per device.

v0:
```python
import jax
import jax.numpy as jnp
from jax import lax
from jax.sharding import PartitionSpec as P

D = 256
HEADS = 4
CAPS = 4
ITERS = 3


def laid_out(tiles, dim):
    tiles = jnp.moveaxis(tiles, 0, dim)
    shape = tiles.shape
    return tiles.reshape(*shape[:dim], shape[dim] * shape[dim + 1], *shape[dim + 2 :])


def gather_packed(arrays, axis, dims):
    vector = jnp.concatenate([a.reshape(-1) for a in arrays])
    lines, at, finished = (lax.all_gather(vector, axis), 0, [])
    for a, dim in zip(arrays, dims):
        tiles = lines[:, at : at + a.size].reshape(-1, *a.shape)
        finished.append(laid_out(tiles, dim))
        at += a.size
    return tuple(finished)


def local_routing(vectors, valid, base):
    user_count, history_len, width_here = vectors.shape
    logits = jnp.broadcast_to(base[None], (user_count, CAPS, history_len))
    capsules = jnp.zeros((user_count, CAPS, width_here), jnp.float32)
    for sweep in range(ITERS):
        weights = jax.nn.softmax(logits, axis=1) * valid[:, None, :]
        summed = jnp.einsum("ukl,uld->ukd", weights, vectors, precision=lax.Precision.HIGHEST)
        squares = jnp.sum(summed * summed, axis=-1)
        factor = jnp.sqrt(squares) / (1.0 + squares)
        capsules = summed * factor[..., None]
        if sweep + 1 < ITERS:
            logits = logits + jnp.einsum(
                "ukd,uld->ukl", capsules, vectors, precision=lax.Precision.HIGHEST
            )
    return capsules


def body(
    features, item_ids, item_table, lengths, routing_seed, w_qkv, w_out, w_bilinear, w_up, w_down
):
    pa_count = lax.axis_size("pa")
    dev_count = lax.axis_size("dev")
    owned_users = lengths.shape[0] // pa_count
    head_size = D // HEADS
    share = owned_users // dev_count
    core = lax.axis_index("dev")

    def pick(array):
        shaped = array.reshape((pa_count, dev_count, share) + array.shape[1:])
        chosen = lax.dynamic_index_in_dim(shaped, core, 1, keepdims=False)
        return chosen.reshape((pa_count * share,) + array.shape[1:])

    features = pick(features)
    item_ids = pick(item_ids)
    lengths = pick(lengths)
    w_qkv, w_out, w_bilinear, w_up, w_down = gather_packed(
        (w_qkv, w_out, w_bilinear, w_up, w_down), "dev", (2, 0, 1, 1, 0)
    )
    own_lens = lax.dynamic_slice_in_dim(lengths, lax.axis_index("pa") * share, share)
    features, item_ids = (
        lax.all_to_all(features, "pa", split_axis=0, concat_axis=1, tiled=True),
        lax.all_to_all(item_ids, "pa", split_axis=0, concat_axis=1, tiled=True),
    )
    user_count, span_here, model_width = features.shape
    heads_here = w_qkv.shape[2] // head_size
    inputs = (
        features.astype(jnp.float32) + jnp.take(item_table, item_ids, axis=0).astype(jnp.float32)
    ).astype(jnp.bfloat16)
    flat_rows = inputs.reshape(-1, model_width)

    def project(index):
        shaped = w_qkv[index].reshape(model_width, heads_here, head_size)
        made = jnp.einsum(
            "nd,dhe->hne", flat_rows, shaped, preferred_element_type=jnp.float32
        ).astype(jnp.bfloat16)
        return made.reshape(heads_here, user_count, span_here, head_size)

    queries = project(0)
    key_block = project(1)
    value_block = project(2)
    score_scale = 1.0 / head_size**0.5
    count_here = key_block.shape[2]
    scores = (
        jnp.einsum("huqe,huke->huqk", queries, key_block, preferred_element_type=jnp.float32)
        * score_scale
    )
    positions = jnp.arange(count_here, dtype=jnp.int32)
    valid_keys = positions[None, :] < own_lens[:, None]
    mask_four = valid_keys[None, :, None, :]
    probs = jnp.where(mask_four, jnp.exp(scores), 0.0)
    totals = jnp.sum(probs, axis=-1)
    weighted = jnp.einsum(
        "huqk,huke->huqe",
        probs.astype(jnp.bfloat16),
        value_block,
        preferred_element_type=jnp.float32,
    )
    attended = (weighted / totals[..., None]).astype(jnp.bfloat16)
    out_heads = w_out.reshape(heads_here, head_size, w_out.shape[1])
    attended_term = jnp.einsum(
        "huqe,hef->uqf", attended, out_heads, preferred_element_type=jnp.float32
    )
    hidden = jax.nn.gelu(jnp.dot(flat_rows, w_up, preferred_element_type=jnp.float32)).astype(
        jnp.bfloat16
    )
    partial_terms = attended_term.reshape(-1, w_out.shape[1]) + jnp.dot(
        hidden, w_down, preferred_element_type=jnp.float32
    )
    interest_in = (
        partial_terms + jnp.dot(flat_rows, w_bilinear, preferred_element_type=jnp.float32)
    ).astype(jnp.bfloat16)
    interest_in = interest_in.reshape(user_count, span_here, -1)
    history_len = interest_in.shape[1]
    valid = (jnp.arange(history_len)[None, :] < own_lens[:, None]).astype(jnp.float32)
    base = (routing_seed.astype(jnp.float32) - 7.5) * 0.25
    routed = local_routing(interest_in.astype(jnp.float32), valid, base)
    capsules = lax.all_to_all(routed, "dev", split_axis=2, concat_axis=0, tiled=True)
    return capsules


def solution(mesh):
    in_specs = (
        P("au", "pa", None),
        P("au", "pa"),
        P(),
        P("au"),
        P(),
        P(None, None, "dev"),
        P("dev", None),
        P(None, "dev"),
        P(None, "dev"),
        P("dev", None),
    )
    out_specs = P(("au", "pa"), None, "dev")
    return jax.shard_map(body, mesh=mesh, in_specs=in_specs, out_specs=out_specs, check_vma=False)
```

profile of v0, /device:TPU:1, one launch (start us, length us, event | category | flops | bytes accessed | tf_op | source)
XLA Modules:
  0.0 140.4 jit_solution(1867006073911560895)
XLA Ops:
  6.5 1.1 constant_dynamic-update-slice_fusion.3
  7.6 0.9 copy.136
  8.5 1.1 copy.137
  9.6 1.2 copy.138
  10.8 0.8 bitcast_dynamic-update-slice_fusion
  11.7 1.0 copy-done.7
  12.7 0.9 reshape.215
  13.6 0.7 reshape.245
  14.3 6.2 %all-to-all-start.1 = ((s32[8,1,512]{2,1,0:T(1,128)}), s32[8,1,512]{2,1,0:T(1,128)S(1)}, u32[]{:S(2)}, u32[]{:S(2)}) async-start(s32[8,1,512]{2,1,0:T(1,128)} %reshape.245), calls=%async_computation.1 | async-start | bytes 32768 | tf_op jit(solution)/shard_map/all_to_all | solution.py:69
  20.5 0.8 reshape.205
  21.5 3.0 %constant_dynamic-slice_fusion.1 = bf16[8,1,64,8,256]{4,3,2,1,0:T(8,128)(2,1)} fusion(bf16[8,2,64,8,256]{4,3,2,1,0:T(8,128)(2,1)} %bitcast.141, s32[]{:T(128)S(6)} %select_n.42), kind=kLoop, calls=%fused_computation.91 | loop fusion | bytes 4194308 | tf_op jit(solution)/shard_map/jit(dynamic_index_in_dim)/dynamic_slice | solution.py:57
  24.6 0.9 all-to-all-done.1
  25.6 4.3 %all-to-all-start = ((bf16[512,8,256]{2,1,0:T(8,128)(2,1)}), bf16[512,8,256]{2,1,0:T(8,128)(2,1)}, u32[]{:S(2)}, u32[]{:S(2)}) async-start(bf16[512,8,256]{2,1,0:T(8,128)(2,1)} %bitcast.131), calls=%async_computation | async-start | bytes 4194304 | tf_op jit(solution)/shard_map/all_to_all | solution.py:68
  29.9 0.5 broadcast.110
  30.4 0.7 reduce.7
  31.6 16.9 %gather_fusion = bf16[4096,256]{1,0:T(8,128)(2,1)} fusion(bf16[4096,256]{1,0:T(8,128)(2,1)S(1)} %copy-done, s32[4096]{0:T(1024)S(1)} %broadcast_clamp_fusion), kind=kCustom, calls=%fused_computation | custom fusion | bytes 4210688 | tf_op jit(solution)/shard_map/jit(_take)/gather | solution.py:74
  48.5 1.9 %reshape.233 = bf16[2,425984]{1,0:T(2,128)(2,1)S(1)} reshape(bf16[851968]{0:T(1024)(128)(2,1)} %all-gather.3.cloned.1.call-done) | data formatting | bytes 3407872 | tf_op jit(solution)/shard_map/all_gather | solution.py:20
  50.4 1.2 copy-done.5
  51.6 1.6 %fusion.67 = (bf16[2,131072]{1,0:T(2,128)(2,1)}, bf16[2,131072]{1,0:T(2,128)(2,1)S(1)}) fusion(bf16[2,425984]{1,0:T(2,128)(2,1)S(1)} %reshape.233), kind=kLoop, calls=%fused_computation.100 | loop fusion | bytes 2097152 | tf_op jit(solution)/shard_map/slice | solution.py:22
  53.1 1.4 %slice_bitcast_fusion = bf16[1,2,768,128]{3,1,2,0:T(2,128)(2,1)S(1)} fusion(bf16[2,425984]{1,0:T(2,128)(2,1)} %copy-done.5), kind=kLoop, calls=%fused_computation.44 | loop fusion | bytes 786432
  54.6 0.8 copy.110
  55.4 0.8 copy.103
  56.3 1.8 %slice_bitcast_fusion.1 = (bf16[1,2,256,128]{3,1,2,0:T(2,128)(2,1)}, bf16[2,32768]{1,0:T(2,128)(2,1)S(1)}) fusion(bf16[2,425984]{1,0:T(2,128)(2,1)} %copy-done.5), kind=kLoop, calls=%fused_computation.51 | loop fusion | bytes 524288
  58.2 1.1 copy.150
  59.3 1.0 copy.117
  60.3 1.1 reshape_reshape.3
  61.4 0.9 copy.151
  62.5 3.0 %fusion.27 = bf16[64,8,8,256]{3,2,0,1:T(8,128)(2,1)S(1)} fusion(bf16[8,64,8,256]{3,2,1,0:T(8,128)(2,1)} %bitcast.36, bf16[64,8,8,256]{3,2,1,0:T(8,128)(2,1)S(1)} %bitcast.130, pred[64,8,8]{2,0,1:T(8,128)(4,1)S(1)} %copy.106), kind=kLoop, calls=%fused_computation.32 | loop fusion | flops 5242880 | bytes 6295552 | tf_op jit(solution)/shard_map/convert_element_type | solution.py:75
  65.8 2.1 %fusion.22 = bf16[4,4096,64]{1,2,0:T(8,128)(2,1)} fusion(bf16[256,4,64]{0,2,1:T(8,128)(2,1)S(1)} %bitcast.147, bf16[4096,256,1]{1,0,2:T(8,128)(2,1)S(1)} %bitcast.125), kind=kOutput, calls=%fused_computation.27 | convolution fusion | flops 537919488 | bytes 4325376 | tf_op jit(solution)/shard_map/nd,dhe->hne/dot_general | solution.py:80
  67.9 4.8 %copy.133 = bf16[4,4096,64]{2,1,0:T(8,128)(2,1)} copy(bf16[4,4096,64]{1,2,0:T(8,128)(2,1)} %fusion.22) | data formatting | bytes 4194304 | tf_op jit(solution)/shard_map/reshape | solution.py:83
  72.7 2.1 %fusion.21 = bf16[4,4096,64]{1,2,0:T(8,128)(2,1)} fusion(bf16[256,4,64]{0,2,1:T(8,128)(2,1)S(1)} %bitcast.146, bf16[4096,256,1]{1,0,2:T(8,128)(2,1)S(1)} %bitcast.126), kind=kOutput, calls=%fused_computation.26 | convolution fusion | flops 537919488 | bytes 4325376 | tf_op jit(solution)/shard_map/nd,dhe->hne/dot_general | solution.py:80
  74.9 4.8 %copy.132 = bf16[4,4096,64]{2,1,0:T(8,128)(2,1)} copy(bf16[4,4096,64]{1,2,0:T(8,128)(2,1)} %fusion.21) | data formatting | bytes 4194304 | tf_op jit(solution)/shard_map/reshape | solution.py:83
  79.6 2.1 %fusion.23 = bf16[4,4096,64]{1,2,0:T(8,128)(2,1)} fusion(bf16[256,4,64]{0,2,1:T(8,128)(2,1)S(1)} %bitcast.145, bf16[4096,256,1]{1,0,2:T(8,128)(2,1)S(1)} %bitcast.127), kind=kOutput, calls=%fused_computation.28 | convolution fusion | flops 537919488 | bytes 4325376 | tf_op jit(solution)/shard_map/nd,dhe->hne/dot_general | solution.py:80
  81.7 4.8 %copy.134 = bf16[4,4096,64]{2,1,0:T(8,128)(2,1)} copy(bf16[4,4096,64]{1,2,0:T(8,128)(2,1)} %fusion.23) | data formatting | bytes 4194304 | tf_op jit(solution)/shard_map/reshape | solution.py:83
  86.6 5.0 %fusion.13 = (f32[4,64,64]{2,1,0:T(8,128)S(1)}, f32[4,64,64,64]{2,3,1,0:T(8,128)S(1)}) fusion(pred[64,64]{1,0:T(8,128)(4,1)S(1)} %get-tuple-element.15, bf16[4,64,64,64]{3,2,1,0:T(8,128)(2,1)} %bitcast.134, bf16[4,64,64,64]{3,2,1,0:T(8,128)(2,1)} %bitcast.133), kind=kOutput, calls=%fused_computation.16 | convolution fusion | flops 137347072 | bytes 8458240 | tf_op jit(solution)/shard_map/huqe,huke->huqk/dot_general | solution.py:91
  91.5 5.3 %fusion.10 = bf16[64,64,64,4]{2,1,0,3:T(8,128)(2,1)S(1)} fusion(f32[64,64,4]{1,0,2:T(8,128)S(1)} %bitcast.156, bf16[4,64,64,64]{3,2,1,0:T(8,128)(2,1)S(1)} %bitcast.135, f32[4,64,64,64]{2,3,1,0:T(8,128)S(1)} %get-tuple-element.17, pred[64,64]{1,0:T(8,128)(4,1)S(1)} %get-tuple-element.15), kind=kOutput, calls=%fused_computation.13 | convolution fusion | flops 139460608 | bytes 8458240 | tf_op jit(solution)/shard_map/huqk,huke->huqe/dot_general | solution.py:99
  96.8 2.8 %convolution_bitcast_fusion = f32[4096,256]{1,0:T(8,128)} fusion(bf16[4096,64,4]{1,0,2:T(8,128)(2,1)S(1)} %bitcast.132, bf16[4,64,256]{2,1,0:T(8,128)(2,1)S(1)} %reshape_reshape_reshape.3), kind=kOutput, calls=%fused_computation.19 | convolution fusion | flops 536870912 | bytes 6422528 | tf_op jit(solution)/shard_map/huqe,hef->uqf/dot_general | solution.py:107
  99.7 9.4 %fusion.15 = f32[4096,256]{1,0:T(8,128)} fusion(f32[4096,256]{1,0:T(8,128)} %convolution_bitcast_fusion, bf16[1024,256]{1,0:T(8,128)(2,1)} %reshape_reshape.3, bf16[4096,256]{1,0:T(8,128)(2,1)S(1)} %bitcast.128, bf16[256,1024]{0,1:T(8,128)(2,1)S(1)} %bitcast.148), kind=kOutput, calls=%fused_computation.20 | convolution fusion | flops 4333764608 | bytes 11534336 | tf_op jit(solution)/shard_map/dot_general | solution.py:113
  109.0 3.6 %fusion.20 = bf16[4096,256]{1,0:T(8,128)(2,1)S(1)} fusion(f32[4096,256]{1,0:T(8,128)} %fusion.15, bf16[4096,256]{1,0:T(8,128)(2,1)} %bitcast.129, bf16[256,256]{0,1:T(8,128)(2,1)S(1)} %bitcast.144), kind=kOutput, calls=%fused_computation.22 | convolution fusion | flops 538968064 | bytes 8519680 | tf_op jit(solution)/shard_map/dot_general | solution.py:117
  112.6 1.0 multiply_reduce_fusion.2
  113.9 1.8 %convolution_add_fusion.2 = f32[64,4,64]{2,1,0:T(4,128)S(1)} fusion(bf16[64,64,256]{2,1,0:T(8,128)(2,1)S(1)} %bitcast.121, f32[64,4,256]{2,1,0:T(4,128)S(1)} %get-tuple-element.19, f32[64,4]{1,0:T(8,128)S(1)} %copy.121, f32[4,64]{1,0:T(4,128)S(1)} %get-tuple-element.12), kind=kOutput, calls=%fused_computation.40 | convolution fusion | flops 50413568 | bytes 2426880 | tf_op jit(solution)/shard_map/ukd,uld->ukl/dot_general | solution.py:39
  115.9 1.0 multiply_reduce_fusion.1
  117.1 3.5 %convolution_add_fusion.1 = f32[64,4,64]{2,1,0:T(4,128)S(1)} fusion(f32[64,4,64]{2,1,0:T(4,128)S(1)} %convolution_add_fusion.2, bf16[64,64,256]{2,1,0:T(8,128)(2,1)} %bitcast.123, f32[64,4,256]{2,1,0:T(4,128)S(1)} %get-tuple-element.23, f32[64,4]{1,0:T(8,128)S(1)} %copy.124), kind=kOutput, calls=%fused_computation.39 | convolution fusion | flops 50413568 | bytes 2491392 | tf_op jit(solution)/shard_map/ukd,uld->ukl/dot_general | solution.py:39
  120.8 2.6 %multiply_reduce_fusion = (f32[64,4]{1,0:T(8,128)S(1)}, f32[64,4,256]{2,1,0:T(4,128)S(1)}) fusion(bf16[64,64,256]{2,1,0:T(8,128)(2,1)} %bitcast.124, f32[64,4,64]{2,1,0:T(4,128)S(1)} %get-tuple-element.25, f32[64,64]{1,0:T(8,128)S(1)} %get-tuple-element.24, f32[64,64]{1,0:T(8,128)S(1)} %get-tuple-element.14), kind=kOutput, calls=%fused_computation.45 | convolution fusion | flops 50495232 | bytes 2458624 | tf_op jit(solution)/shard_map/ukl,uld->ukd/dot_general | solution.py:34
  124.6 5.7 %all_to_all.46 = f32[2,1,32768]{2,1,0:T(1,128)S(1)} all-to-all(f32[2,1,32768]{2,1,0:T(1,128)S(1)} %reshape.247), channel_id=1, replica_groups=mesh['au'=8,'pa'=8,'dev'=2] {'dev'}, dimensions={0} | all-to-all | bytes 524288 | tf_op jit(solution)/shard_map/all_to_all | solution.py:124
  130.2 0.5 broadcast.111
  130.8 1.4 %reduce.8 = f32[2,32768]{1,0:T(2,128)S(1)} reduce(f32[2,1,32768]{2,1,0:T(1,128)S(1)} %all_to_all.46, f32[]{:T(128)} %broadcast.111), dimensions={1}, to_apply=%all_to_all.39.reduce_sub_computation | reduce | bytes 524292 | tf_op jit(solution)/shard_map/all_to_all | solution.py:124
  132.6 0.9 copy.129
  (65 shorter events, 3.8 us)
Async XLA Ops:
  6.5 25.0 %copy-start = (bf16[4096,256]{1,0:T(8,128)(2,1)S(1)}, bf16[4096,256]{1,0:T(8,128)(2,1)}, u32[]{:S(2)}) copy-start(bf16[4096,256]{1,0:T(8,128)(2,1)} %param.12) | copy-start | bytes 6291460
  6.5 18.0 %copy-start.11 = (s32[4,64]{1,0:T(4,128)S(1)}, s32[4,64]{1,0:T(4,128)}, u32[]{:S(2)}) copy-start(s32[4,64]{1,0:T(4,128)} %param.14) | copy-start | bytes 3076
  6.5 42.0 %all-gather.3.cloned.1.call-start = ((), (), s32[]{:S(2)}) async-start(), calls=%async_computation.3 | async-start | bytes 2555904 | tf_op jit(solution)/shard_map/all_gather | solution.py:20
  11.7 1.0 copy-start.7
  14.3 11.2 %all-to-all-start.1 = ((s32[8,1,512]{2,1,0:T(1,128)}), s32[8,1,512]{2,1,0:T(1,128)S(1)}, u32[]{:S(2)}, u32[]{:S(2)}) async-start(s32[8,1,512]{2,1,0:T(1,128)} %reshape.245), calls=%async_computation.1 | async-start | bytes 32768 | tf_op jit(solution)/shard_map/all_to_all | solution.py:69
  25.6 36.9 %all-to-all-start = ((bf16[512,8,256]{2,1,0:T(8,128)(2,1)}), bf16[512,8,256]{2,1,0:T(8,128)(2,1)}, u32[]{:S(2)}, u32[]{:S(2)}) async-start(bf16[512,8,256]{2,1,0:T(8,128)(2,1)} %bitcast.131), calls=%async_computation | async-start | bytes 4194304 | tf_op jit(solution)/shard_map/all_to_all | solution.py:68
  50.4 1.2 copy-start.5
  53.1 9.3 %copy-start.4 = (bf16[4096,256]{1,0:T(8,128)(2,1)S(1)}, bf16[4096,256]{1,0:T(8,128)(2,1)}, u32[]{:S(2)}) copy-start(bf16[4096,256]{1,0:T(8,128)(2,1)} %gather_fusion) | copy-start | bytes 6291460
  62.5 3.3 %copy-start.9 = (bf16[1,256,2,128]{1,3,2,0:T(8,128)(2,1)S(1)}, bf16[1,256,2,128]{1,3,2,0:T(8,128)(2,1)}, u32[]{:S(2)}) copy-start(bf16[1,256,2,128]{1,3,2,0:T(8,128)(2,1)} %copy.110) | copy-start | bytes 393220
  65.8 33.8 %copy-start.3 = (bf16[64,8,8,256]{3,2,1,0:T(8,128)(2,1)}, bf16[64,8,8,256]{3,2,1,0:T(8,128)(2,1)S(1)}, u32[]{:S(2)}) copy-start(bf16[64,8,8,256]{3,2,1,0:T(8,128)(2,1)S(1)} %copy.109) | copy-start | bytes 6291460
  67.9 4.8 %copy-start.8 = (bf16[1,256,2,128]{1,3,2,0:T(8,128)(2,1)S(1)}, bf16[1,256,2,128]{1,3,2,0:T(8,128)(2,1)}, u32[]{:S(2)}) copy-start(bf16[1,256,2,128]{1,3,2,0:T(8,128)(2,1)} %copy.103) | copy-start | bytes 393220
  86.6 5.0 %copy-start.6 = (bf16[4,4096,64]{2,1,0:T(8,128)(2,1)S(1)}, bf16[4,4096,64]{2,1,0:T(8,128)(2,1)}, u32[]{:S(2)}) copy-start(bf16[4,4096,64]{2,1,0:T(8,128)(2,1)} %copy.134) | copy-start | bytes 6291460
  96.8 2.9 %copy-start.10 = (bf16[256,2,512]{0,2,1:T(8,128)(2,1)S(1)}, bf16[256,2,512]{0,2,1:T(8,128)(2,1)}, u32[]{:S(2)}) copy-start(bf16[256,2,512]{0,2,1:T(8,128)(2,1)} %copy.117) | copy-start | bytes 1572868
  112.6 3.2 %copy-start.2 = (bf16[4096,256]{1,0:T(8,128)(2,1)}, bf16[4096,256]{1,0:T(8,128)(2,1)S(1)}, u32[]{:S(2)}) copy-start(bf16[4096,256]{1,0:T(8,128)(2,1)S(1)} %fusion.20) | copy-start | bytes 6291460
  117.1 16.5 %copy-start.1 = (bf16[4096,256]{1,0:T(8,128)(2,1)S(1)}, bf16[4096,256]{1,0:T(8,128)(2,1)}, u32[]{:S(2)}) copy-start(bf16[4096,256]{1,0:T(8,128)(2,1)} %param.12) | copy-start | bytes 6291460
Sparse Core Ops, SparseCore 0:
  12.8 16.3 all-gather.2
where the time goes:
time: 141 us; the launch traced here: 140 us
  local copies, waits for them, and re-layouts  61.2 us (43%)
  matrix products  42.4 us (30%)
  between operations  13.8 us (10%)
  starting transfers between devices  10.5 us (7%)
  other arithmetic  5.86 us (4%)
  blocking collectives  5.69 us (4%)
    gather x1, local copies, waits for them, and re-layouts, body(): jnp.take(item_table, item_ids, axis=0).astype(jnp.float32)  16.9 us
    reshape x3, local copies, waits for them, and re-layouts, project(): return made.reshape(heads_here, user_count, span_here, head_size)  14.4 us
    unnamed x40, local copies, waits for them, and re-layouts  14.3 us
    dot_general x1, matrix products, body(): jnp.dot(hidden, w_down, preferred_element_type=jnp.float32)  9.38 us
    dot_general x3, matrix products, project(): jnp.einsum('nd,dhe->hne', flat_rows, shaped, preferred_element_type=jnp.f...  6.29 us
    all_to_all x1, starting transfers between devices, body(): lax.all_to_all(item_ids, 'pa', split_axis=0, concat_axis=1, tiled=True)  6.2 us
    all_to_all x1, blocking collectives, body(): lax.all_to_all(routed, 'dev', split_axis=2, concat_axis=0, tiled=True)  5.69 us
    dot_general x2, matrix products, local_routing(): jnp.einsum('ukd,uld->ukl', capsules, vectors, precision=lax.Precision.HIG...  5.34 us
  transfers between devices with their start and end apart: 3, of which 1 were waited for; matrix products, arithmetic and copies ran while one was open for 26% of the time, Pallas kernels for 0%

commit v1 on v0

--- a/solution.py
+++ b/solution.py
@@ -65,7 +65,10 @@
     )
     own_lens = lax.dynamic_slice_in_dim(lengths, lax.axis_index("pa") * share, share)
     features, item_ids = (
-        lax.all_to_all(features, "pa", split_axis=0, concat_axis=1, tiled=True),
+        jnp.concatenate(
+            lax.all_to_all(jnp.stack(jnp.split(features, lax.axis_size("pa"), axis=0)), "pa", 0, 0),
+            axis=1,
+        ),
         lax.all_to_all(item_ids, "pa", split_axis=0, concat_axis=1, tiled=True),
     )
     user_count, span_here, model_width = features.shape

time: 141 us -> 144 us (1.021)
  matrix products: 42.4 us -> 38.9 us
  local copies, waits for them, and re-layouts: 61.2 us -> 64.7 us
  waiting for transfers between devices: 0.95 us -> 3.22 us
    unnamed x40 -> x41, local copies, waits for them, and re-layouts: 14.3 us -> 20 us
    all_to_all x1, waiting for transfers between devices: 0.01 us -> 3.2 us  [body(): lax.all_to_all(jnp.stack(jnp.split(features, lax.axis_size('pa'), axis=0)...]
    dynamic_slice x4 -> x3, local copies, waits for them, and re-layouts: 3.08 us -> 0.06 us  [pick(): chosen = lax.dynamic_index_in_dim(shaped, core, 1, keepdims=False)]
    dot_general x2, matrix products: 5.34 us -> 3.61 us  [local_routing(): jnp.einsum('ukd,uld->ukl', capsules, vectors, precision=lax.Precision.HIG...]
    another operation x0 -> x1, local copies, waits for them, and re-layouts: none -> 1.7 us  [body(): jnp.stack(jnp.split(features, lax.axis_size('pa'), axis=0))]
    dot_general x3, matrix products: 4.73 us -> 3.14 us  [local_routing(): jnp.einsum('ukl,uld->ukd', weights, vectors, precision=lax.Precision.HIGH...]
    slice x4, local copies, waits for them, and re-layouts: 1.66 us -> 3.21 us  [project(): shaped = w_qkv[index].reshape(model_width, heads_here, head_size)]
  transfers between devices with their start and end apart: 3 -> 3, of which waited for: 1 -> 1; matrix products, arithmetic and copies ran while one was open for 26% -> 32% of each run, Pallas kernels for 0% -> 0%
where the time goes in v1:
time: 144 us; the launch traced here: 143 us
  local copies, waits for them, and re-layouts  64.7 us (45%)
  matrix products  38.9 us (27%)
  between operations  13.7 us (10%)
  starting transfers between devices  11.3 us (8%)
  other arithmetic  5.57 us (4%)
  blocking collectives  5.49 us (4%)
  waiting for transfers between devices  3.22 us (2%)
    unnamed x41, local copies, waits for them, and re-layouts  20 us
    gather x1, local copies, waits for them, and re-layouts, body(): jnp.take(item_table, item_ids, axis=0).astype(jnp.float32)  16.9 us
    reshape x3, local copies, waits for them, and re-layouts, project(): return made.reshape(heads_here, user_count, span_here, head_size)  14.4 us
    dot_general x1, matrix products, body(): jnp.dot(hidden, w_down, preferred_element_type=jnp.float32)  9.2 us
    dot_general x3, matrix products, project(): jnp.einsum('nd,dhe->hne', flat_rows, shaped, preferred_element_type=jnp.f...  6.29 us
    all_to_all x1, starting transfers between devices, body(): lax.all_to_all(item_ids, 'pa', split_axis=0, concat_axis=1, tiled=True)  6.2 us
    all_to_all x1, blocking collectives, body(): lax.all_to_all(routed, 'dev', split_axis=2, concat_axis=0, tiled=True)  5.49 us
    dot_general x1, matrix products, body(): jnp.einsum('huqk,huke->huqe', probs.astype(jnp.bfloat16), value_block, pr...  5.27 us
  transfers between devices with their start and end apart: 3, of which 1 were waited for; matrix products, arithmetic and copies ran while one was open for 32% of the time, Pallas kernels for 0%

profile of v1, /device:TPU:1, one launch (start us, length us, event | category | flops | bytes accessed | tf_op | source)
XLA Modules:
  0.0 142.9 jit_solution(12511521837547818165)
XLA Ops:
  6.5 1.0 reshape.228
  7.6 0.7 reshape.257
  8.3 6.2 %all-to-all-start.1 = ((s32[8,1,512]{2,1,0:T(1,128)}), s32[8,1,512]{2,1,0:T(1,128)S(1)}, u32[]{:S(2)}, u32[]{:S(2)}) async-start(s32[8,1,512]{2,1,0:T(1,128)} %reshape.257), calls=%async_computation.1 | async-start | bytes 32768 | tf_op jit(solution)/shard_map/all_to_all | solution.py:72
  14.6 0.9 constant_dynamic-update-slice_fusion
  15.5 0.9 copy.159
  16.4 1.1 copy.160
  17.5 1.2 copy.161
  18.6 0.8 bitcast_dynamic-update-slice_fusion
  19.5 1.0 copy-done.4
  20.6 1.7 %fusion.43 = bf16[8,64,8,256]{3,2,1,0:T(8,128)(2,1)} fusion(bf16[8,2,64,8,256]{4,3,2,1,0:T(8,128)(2,1)} %bitcast.165, s32[]{:T(128)S(6)} %select_n.42), kind=kLoop, calls=%fused_computation.58 | loop fusion | bytes 524292
  22.4 1.7 %fusion.42 = bf16[8,64,8,256]{3,2,1,0:T(8,128)(2,1)} fusion(bf16[8,64,8,256]{3,2,1,0:T(8,128)(2,1)} %fusion.43, bf16[8,2,64,8,256]{4,3,2,1,0:T(8,128)(2,1)} %bitcast.166, s32[]{:T(128)S(6)} %add.104, s32[]{:T(128)S(6)} %select_n.42), kind=kLoop, calls=%fused_computation.56 | loop fusion | bytes 524296
  24.1 1.7 %fusion.41 = bf16[8,64,8,256]{3,2,1,0:T(8,128)(2,1)} fusion(bf16[8,64,8,256]{3,2,1,0:T(8,128)(2,1)} %fusion.42, bf16[8,2,64,8,256]{4,3,2,1,0:T(8,128)(2,1)} %bitcast.167, s32[]{:T(128)S(6)} %add.105, s32[]{:T(128)S(6)} %select_n.42), kind=kLoop, calls=%fused_computation.54 | loop fusion | bytes 524296
  25.8 1.7 %fusion.40 = bf16[8,64,8,256]{3,2,1,0:T(8,128)(2,1)} fusion(bf16[8,64,8,256]{3,2,1,0:T(8,128)(2,1)} %fusion.41, bf16[8,2,64,8,256]{4,3,2,1,0:T(8,128)(2,1)} %bitcast.168, s32[]{:T(128)S(6)} %add.106, s32[]{:T(128)S(6)} %select_n.42), kind=kLoop, calls=%fused_computation.52 | loop fusion | bytes 524296
  27.5 1.7 %fusion.39 = bf16[8,64,8,256]{3,2,1,0:T(8,128)(2,1)} fusion(bf16[8,64,8,256]{3,2,1,0:T(8,128)(2,1)} %fusion.40, bf16[8,2,64,8,256]{4,3,2,1,0:T(8,128)(2,1)} %bitcast.169, s32[]{:T(128)S(6)} %add.107, s32[]{:T(128)S(6)} %select_n.42), kind=kLoop, calls=%fused_computation.50 | loop fusion | bytes 524296
  29.2 1.7 %fusion.38 = bf16[8,64,8,256]{3,2,1,0:T(8,128)(2,1)} fusion(bf16[8,64,8,256]{3,2,1,0:T(8,128)(2,1)} %fusion.39, bf16[8,2,64,8,256]{4,3,2,1,0:T(8,128)(2,1)} %bitcast.170, s32[]{:T(128)S(6)} %add.108, s32[]{:T(128)S(6)} %select_n.42), kind=kLoop, calls=%fused_computation.48 | loop fusion | bytes 524296
  30.9 1.7 %fusion.37 = bf16[8,64,8,256]{3,2,1,0:T(8,128)(2,1)} fusion(bf16[8,64,8,256]{3,2,1,0:T(8,128)(2,1)} %fusion.38, bf16[8,2,64,8,256]{4,3,2,1,0:T(8,128)(2,1)} %bitcast.171, s32[]{:T(128)S(6)} %add.109, s32[]{:T(128)S(6)} %select_n.42), kind=kLoop, calls=%fused_computation.46 | loop fusion | bytes 524296
  32.6 1.7 %fusion.36 = bf16[8,64,8,256]{3,2,1,0:T(8,128)(2,1)} fusion(bf16[8,64,8,256]{3,2,1,0:T(8,128)(2,1)} %fusion.37, bf16[8,2,64,8,256]{4,3,2,1,0:T(8,128)(2,1)} %bitcast.172, s32[]{:T(128)S(6)} %add.110, s32[]{:T(128)S(6)} %select_n.42), kind=kLoop, calls=%fused_computation.44 | loop fusion | bytes 524296 | tf_op jit(solution)/shard_map/stack | solution.py:69
  34.4 5.1 %all-to-all-start = ((bf16[8,64,8,256]{3,2,1,0:T(8,128)(2,1)}), bf16[8,64,8,256]{3,2,1,0:T(8,128)(2,1)}, u32[]{:S(2)}, u32[]{:S(2)}) async-start(bf16[8,64,8,256]{3,2,1,0:T(8,128)(2,1)} %fusion.36), calls=%async_computation | async-start | bytes 4194304 | tf_op jit(solution)/shard_map/all_to_all | solution.py:69
  39.5 0.5 broadcast.110
  40.0 0.7 reduce.7
  41.2 16.9 %gather_fusion = bf16[4096,256]{1,0:T(8,128)(2,1)} fusion(bf16[4096,256]{1,0:T(8,128)(2,1)S(1)} %copy-done, s32[4096]{0:T(1024)S(1)} %broadcast_clamp_fusion), kind=kCustom, calls=%fused_computation | custom fusion | bytes 4210688 | tf_op jit(solution)/shard_map/jit(_take)/gather | solution.py:77
  58.1 1.9 %reshape.245 = bf16[2,425984]{1,0:T(2,128)(2,1)S(1)} reshape(bf16[851968]{0:T(1024)(128)(2,1)} %all-gather.3.cloned.1.call-done) | data formatting | bytes 3407872 | tf_op jit(solution)/shard_map/all_gather | solution.py:20
  60.0 0.7 fusion.74
  61.1 0.7 fusion.75
  61.8 1.6 %copy.134 = bf16[1,256,2,128]{1,3,2,0:T(8,128)(2,1)} copy(bf16[1,256,2,128]{3,1,0,2:T(8,128)(2,1)} %get-tuple-element.10) | data formatting | bytes 262144 | tf_op jit(solution)/shard_map/slice | solution.py:82
  63.4 0.8 copy.129
  64.9 1.1 reshape_reshape.3
  66.1 3.2 %all-to-all-done = bf16[8,64,8,256]{3,2,1,0:T(8,128)(2,1)} async-done(((bf16[8,64,8,256]{3,2,1,0:T(8,128)(2,1)}), bf16[8,64,8,256]{3,2,1,0:T(8,128)(2,1)}, u32[]{:S(2)}, u32[]{:S(2)}) %all-to-all-start) | async-done | bytes 2097184 | tf_op jit(solution)/shard_map/all_to_all | solution.py:69
  69.3 2.8 %fusion.26 = bf16[64,8,8,256]{3,2,1,0:T(8,128)(2,1)S(1)} fusion(bf16[8,64,8,256]{3,2,1,0:T(8,128)(2,1)} %all-to-all-done, bf16[64,8,8,256]{3,2,1,0:T(8,128)(2,1)} %bitcast.155, pred[64,8,8]{2,1,0:T(8,128)(4,1)S(1)} %copy.132), kind=kLoop, calls=%fused_computation.31 | loop fusion | flops 5242880 | bytes 6295552 | tf_op jit(solution)/shard_map/convert_element_type | solution.py:78
  72.1 2.1 %fusion.22 = bf16[4,4096,64]{1,2,0:T(8,128)(2,1)} fusion(bf16[256,4,64]{0,2,1:T(8,128)(2,1)S(1)} %bitcast.178, bf16[4096,256,1]{1,0,2:T(8,128)(2,1)S(1)} %bitcast.150), kind=kOutput, calls=%fused_computation.27 | convolution fusion | flops 537919488 | bytes 4325376 | tf_op jit(solution)/shard_map/nd,dhe->hne/dot_general | solution.py:83
  74.2 4.8 %copy.157 = bf16[4,4096,64]{2,1,0:T(8,128)(2,1)} copy(bf16[4,4096,64]{1,2,0:T(8,128)(2,1)} %fusion.22) | data formatting | bytes 4194304 | tf_op jit(solution)/shard_map/reshape | solution.py:86
  79.0 2.1 %fusion.21 = bf16[4,4096,64]{1,2,0:T(8,128)(2,1)} fusion(bf16[256,4,64]{0,2,1:T(8,128)(2,1)S(1)} %bitcast.177, bf16[4096,256,1]{1,0,2:T(8,128)(2,1)S(1)} %bitcast.151), kind=kOutput, calls=%fused_computation.26 | convolution fusion | flops 537919488 | bytes 4325376 | tf_op jit(solution)/shard_map/nd,dhe->hne/dot_general | solution.py:83
  81.1 4.8 %copy.156 = bf16[4,4096,64]{2,1,0:T(8,128)(2,1)} copy(bf16[4,4096,64]{1,2,0:T(8,128)(2,1)} %fusion.21) | data formatting | bytes 4194304 | tf_op jit(solution)/shard_map/reshape | solution.py:86
  85.9 2.1 %fusion.23 = bf16[4,4096,64]{1,2,0:T(8,128)(2,1)} fusion(bf16[256,4,64]{0,2,1:T(8,128)(2,1)S(1)} %bitcast.176, bf16[4096,256,1]{1,0,2:T(8,128)(2,1)S(1)} %bitcast.152), kind=kOutput, calls=%fused_computation.28 | convolution fusion | flops 537919488 | bytes 4325376 | tf_op jit(solution)/shard_map/nd,dhe->hne/dot_general | solution.py:83
  88.0 4.8 %copy.158 = bf16[4,4096,64]{2,1,0:T(8,128)(2,1)} copy(bf16[4,4096,64]{1,2,0:T(8,128)(2,1)} %fusion.23) | data formatting | bytes 4194304 | tf_op jit(solution)/shard_map/reshape | solution.py:86
  92.8 5.0 %fusion.13 = (f32[4,64,64]{2,1,0:T(8,128)S(1)}, f32[4,64,64,64]{2,3,1,0:T(8,128)S(1)}) fusion(pred[64,64]{1,0:T(8,128)(4,1)S(1)} %get-tuple-element.15, bf16[4,64,64,64]{3,2,1,0:T(8,128)(2,1)} %bitcast.158, bf16[4,64,64,64]{3,2,1,0:T(8,128)(2,1)} %bitcast.157), kind=kOutput, calls=%fused_computation.16 | convolution fusion | flops 137347072 | bytes 8458240 | tf_op jit(solution)/shard_map/huqe,huke->huqk/dot_general | solution.py:94
  97.8 5.3 %fusion.10 = bf16[64,64,64,4]{2,1,0,3:T(8,128)(2,1)S(1)} fusion(f32[64,64,4]{1,0,2:T(8,128)S(1)} %bitcast.187, bf16[4,64,64,64]{3,2,1,0:T(8,128)(2,1)S(1)} %bitcast.159, f32[4,64,64,64]{2,3,1,0:T(8,128)S(1)} %get-tuple-element.17, pred[64,64]{1,0:T(8,128)(4,1)S(1)} %get-tuple-element.15), kind=kOutput, calls=%fused_computation.13 | convolution fusion | flops 139460608 | bytes 8458240 | tf_op jit(solution)/shard_map/huqk,huke->huqe/dot_general | solution.py:102
  103.1 2.8 %convolution_bitcast_fusion = f32[4096,256]{1,0:T(8,128)} fusion(bf16[4096,64,4]{1,0,2:T(8,128)(2,1)S(1)} %bitcast.156, bf16[4,64,256]{2,1,0:T(8,128)(2,1)S(1)} %reshape_reshape_reshape.3), kind=kOutput, calls=%fused_computation.19 | convolution fusion | flops 536870912 | bytes 6422528 | tf_op jit(solution)/shard_map/huqe,hef->uqf/dot_general | solution.py:110
  105.9 9.2 %fusion.15 = f32[4096,256]{1,0:T(8,128)} fusion(f32[4096,256]{1,0:T(8,128)} %convolution_bitcast_fusion, bf16[1024,256]{1,0:T(8,128)(2,1)} %reshape_reshape.3, bf16[4096,256]{1,0:T(8,128)(2,1)S(1)} %bitcast.153, bf16[256,1024]{0,1:T(8,128)(2,1)S(1)} %bitcast.179), kind=kOutput, calls=%fused_computation.20 | convolution fusion | flops 4333764608 | bytes 11534336 | tf_op jit(solution)/shard_map/dot_general | solution.py:116
  115.1 3.6 %fusion.20 = bf16[4096,256]{1,0:T(8,128)(2,1)S(1)} fusion(f32[4096,256]{1,0:T(8,128)} %fusion.15, bf16[4096,256]{1,0:T(8,128)(2,1)} %bitcast.154, bf16[256,256]{0,1:T(8,128)(2,1)S(1)} %bitcast.175), kind=kOutput, calls=%fused_computation.22 | convolution fusion | flops 538968064 | bytes 8519680 | tf_op jit(solution)/shard_map/dot_general | solution.py:120
  118.7 1.0 multiply_reduce_fusion.2
  119.9 1.8 %convolution_add_fusion.2 = f32[64,4,64]{2,1,0:T(4,128)S(1)} fusion(bf16[64,64,256]{2,1,0:T(8,128)(2,1)S(1)} %bitcast.146, f32[64,4,256]{2,1,0:T(4,128)S(1)} %get-tuple-element.19, f32[64,4]{1,0:T(8,128)S(1)} %copy.145, f32[4,64]{1,0:T(4,128)S(1)} %get-tuple-element.12), kind=kOutput, calls=%fused_computation.38 | convolution fusion | flops 50413568 | bytes 2426880 | tf_op jit(solution)/shard_map/ukd,uld->ukl/dot_general | solution.py:39
  121.9 1.0 multiply_reduce_fusion.1
  123.2 1.8 %convolution_add_fusion.1 = f32[64,4,64]{2,1,0:T(4,128)S(1)} fusion(f32[64,4,64]{2,1,0:T(4,128)S(1)} %convolution_add_fusion.2, bf16[64,64,256]{2,1,0:T(8,128)(2,1)S(1)} %bitcast.148, f32[64,4,256]{2,1,0:T(4,128)S(1)} %get-tuple-element.23, f32[64,4]{1,0:T(8,128)S(1)} %copy.148), kind=kOutput, calls=%fused_computation.37 | convolution fusion | flops 50413568 | bytes 2491392 | tf_op jit(solution)/shard_map/ukd,uld->ukl/dot_general | solution.py:39
  125.1 1.0 multiply_reduce_fusion
  127.3 5.5 %all_to_all.42 = f32[2,1,32768]{2,1,0:T(1,128)S(1)} all-to-all(f32[2,1,32768]{2,1,0:T(1,128)S(1)} %reshape.259), channel_id=1, replica_groups=mesh['au'=8,'pa'=8,'dev'=2] {'dev'}, dimensions={0} | all-to-all | bytes 524288 | tf_op jit(solution)/shard_map/all_to_all | solution.py:127
  133.3 1.4 %reduce.8 = f32[2,32768]{1,0:T(2,128)S(1)} reduce(f32[2,1,32768]{2,1,0:T(1,128)S(1)} %all_to_all.42, f32[]{:T(128)} %broadcast.111), dimensions={1}, to_apply=%all_to_all.35.reduce_sub_computation | reduce | bytes 524292 | tf_op jit(solution)/shard_map/all_to_all | solution.py:127
  135.2 0.9 copy.153
  (65 shorter events, 4.8 us)
Async XLA Ops:
  6.5 34.6 %copy-start = (bf16[4096,256]{1,0:T(8,128)(2,1)S(1)}, bf16[4096,256]{1,0:T(8,128)(2,1)}, u32[]{:S(2)}) copy-start(bf16[4096,256]{1,0:T(8,128)(2,1)} %param.12) | copy-start | bytes 6291460
  8.3 26.1 %all-to-all-start.1 = ((s32[8,1,512]{2,1,0:T(1,128)}), s32[8,1,512]{2,1,0:T(1,128)S(1)}, u32[]{:S(2)}, u32[]{:S(2)}) async-start(s32[8,1,512]{2,1,0:T(1,128)} %reshape.257), calls=%async_computation.1 | async-start | bytes 32768 | tf_op jit(solution)/shard_map/all_to_all | solution.py:72
  14.5 43.6 %all-gather.3.cloned.1.call-start = ((), (), s32[]{:S(2)}) async-start(), calls=%async_computation.3 | async-start | bytes 2555904 | tf_op jit(solution)/shard_map/all_gather | solution.py:20
  14.5 7.7 %copy-start.7 = (s32[1024]{0:T(1024)S(1)}, s32[1024]{0:T(1024)}, u32[]{:S(2)}) copy-start(s32[1024]{0:T(1024)} %param.13) | copy-start | bytes 12292
  19.5 1.0 copy-start.4
  20.6 13.7 %copy-start.8 = (s32[4,64]{1,0:T(4,128)S(1)}, s32[4,64]{1,0:T(4,128)}, u32[]{:S(2)}) copy-start(s32[4,64]{1,0:T(4,128)} %param.14) | copy-start | bytes 3076
  34.4 34.9 %all-to-all-start = ((bf16[8,64,8,256]{3,2,1,0:T(8,128)(2,1)}), bf16[8,64,8,256]{3,2,1,0:T(8,128)(2,1)}, u32[]{:S(2)}, u32[]{:S(2)}) async-start(bf16[8,64,8,256]{3,2,1,0:T(8,128)(2,1)} %fusion.36), calls=%async_computation | async-start | bytes 4194304 | tf_op jit(solution)/shard_map/all_to_all | solution.py:69
  69.3 2.8 %copy-start.6 = (bf16[1,256,2,128]{1,3,2,0:T(8,128)(2,1)S(1)}, bf16[1,256,2,128]{1,3,2,0:T(8,128)(2,1)}, u32[]{:S(2)}) copy-start(bf16[1,256,2,128]{1,3,2,0:T(8,128)(2,1)} %copy.134) | copy-start | bytes 393220
  72.1 33.8 %copy-start.2 = (bf16[64,8,8,256]{3,2,1,0:T(8,128)(2,1)}, bf16[64,8,8,256]{3,2,1,0:T(8,128)(2,1)S(1)}, u32[]{:S(2)}) copy-start(bf16[64,8,8,256]{3,2,1,0:T(8,128)(2,1)S(1)} %fusion.26) | copy-start | bytes 6291460
  74.2 4.8 %copy-start.5 = (bf16[1,256,2,128]{1,3,2,0:T(8,128)(2,1)S(1)}, bf16[1,256,2,128]{1,3,2,0:T(8,128)(2,1)}, u32[]{:S(2)}) copy-start(bf16[1,256,2,128]{1,3,2,0:T(8,128)(2,1)} %copy.129) | copy-start | bytes 393220
  92.8 5.0 %copy-start.3 = (bf16[4,4096,64]{2,1,0:T(8,128)(2,1)S(1)}, bf16[4,4096,64]{2,1,0:T(8,128)(2,1)}, u32[]{:S(2)}) copy-start(bf16[4,4096,64]{2,1,0:T(8,128)(2,1)} %copy.158) | copy-start | bytes 6291460
  126.4 9.7 %copy-start.1 = (bf16[4096,256]{1,0:T(8,128)(2,1)S(1)}, bf16[4096,256]{1,0:T(8,128)(2,1)}, u32[]{:S(2)}) copy-start(bf16[4096,256]{1,0:T(8,128)(2,1)} %param.12) | copy-start | bytes 6291460
Sparse Core Ops, SparseCore 0:
  20.7 15.7 all-gather.2
